TPU v7x, 256 devices: a whole 4x4x8 slice. The times are simulated.
256 devices in a mesh: batch: 64 (over y, z, core), feat: 4 (over x).
Axes of the slice: x: 4, y: 4, z: 8, core: 2. Of those that a mesh axis runs over, the one named last changes fastest.
Arguments:
- tables: bfloat16 [4, 128, 2048, 192], P('feat', 'batch'), may hold values from -3 to 3
- bag_ids: int32 [4, 128, 4, 8192], P('feat', 'batch'), may hold values from 0 to 2047
- bag_lengths: int32 [4, 128, 8192], P('feat', 'batch'), may hold values from 1 to 4
- pair_groups: int32 [16, 2], replicated, may hold values from 0 to 15
- compress: bfloat16 [16, 32, 8], P('feat'), may hold values from -1 to 1
- w_hidden: bfloat16 [16, 32, 8, 4096], P('feat'), may hold values from -0.09375 to 0.09375
- hidden_bias: float32 [4096], replicated, may hold values from -4 to 4
- norm_gain: float32 [4096], P('feat'), may hold values from 0.1 to 1.9
Outputs:
- interacted: bfloat16 [8192, 4096], P('batch', 'feat')
Inputs may be any that keep to these rules, and one draw needn't show every extreme that they name: `bag_lengths`: ids at slots from a bag's length on are ignored.
All inputs are finite; a program needn't handle non-finite values.
Results may differ from a plain program's by a relative error of at most 0.0052.
Values may be sent and summed in bfloat16 or wider, within the bound.
A program may use at most 128 MiB of HBM per device.

v0:
```python
import jax
import jax.numpy as jnp
from jax import lax
from jax.sharding import PartitionSpec as P


def take_rows(table_one, ids_one):
    return jnp.take(table_one, ids_one, axis=0)


def select_groups(source, pair_list, group_size):
    offsets = jnp.arange(group_size, dtype=jnp.int32)
    wanted = pair_list[:, :, None] * group_size + offsets[None, None, :]
    shape_out = (pair_list.shape[0], 2, group_size, source.shape[1], source.shape[2])
    return jnp.take(source, wanted.reshape(-1), axis=0).reshape(shape_out)


def squeeze_pairs(chosen, weights):
    row_blocks = chosen[:, 0]
    col_blocks = chosen[:, 1]
    gram_scale = float(chosen.shape[4]) ** (-0.5)
    gram_blocks = (
        jnp.einsum("qfbd,qgbd->qbfg", row_blocks, col_blocks, preferred_element_type=jnp.float32)
        * gram_scale
    )
    squeezed = jnp.einsum(
        "qbfg,qgk->bqfk", gram_blocks, weights.astype(jnp.float32), precision=lax.Precision.HIGHEST
    )
    return squeezed.astype(jnp.bfloat16)


def body(tables, bag_ids, bag_lengths, pair_groups, compress, w_hidden, hidden_bias, norm_gain):
    own_tables = tables[0]
    own_ids = bag_ids[0]
    own_lengths = bag_lengths[0]
    slot_count = own_ids.shape[1]
    pooled_sum = jnp.zeros((own_ids.shape[0], own_ids.shape[2], own_tables.shape[2]), jnp.float32)
    for slot in range(slot_count):
        looked = jax.vmap(take_rows)(own_tables, own_ids[:, slot, :])
        live = (own_lengths > slot)[:, :, None]
        pooled_sum = pooled_sum + jnp.where(live, looked.astype(jnp.float32), 0.0)
    pooled = pooled_sum.astype(jnp.bfloat16)
    feature_tile = lax.all_to_all(pooled, "batch", split_axis=1, concat_axis=0, tiled=True)
    samples = feature_tile.shape[1]
    pair_count = compress.shape[0]
    group_size = compress.shape[1]
    first_pair = lax.axis_index("feat") * pair_count
    local_pairs = lax.dynamic_slice_in_dim(pair_groups, first_pair, pair_count, 0)
    everything = lax.all_gather(feature_tile, "feat", axis=0, tiled=True)
    squeezed = squeeze_pairs(select_groups(everything, local_pairs, group_size), compress)
    squeezed = squeezed.reshape(samples, -1)
    w_flat = w_hidden.reshape(-1, w_hidden.shape[3])
    hid_local = norm_gain.shape[0]
    hid_total = hid_local * lax.axis_size("feat")
    own_start = lax.axis_index("feat") * hid_local
    hidden = lax.psum_scatter(
        lax.dot_general(
            w_flat, squeezed, (((0,), (1,)), ((), ())), preferred_element_type=jnp.float32
        ),
        "feat",
        scatter_dimension=0,
        tiled=True,
    )
    local_bias = lax.dynamic_slice_in_dim(hidden_bias, own_start, hid_local, 0)
    hidden = hidden + local_bias[:, None]
    row_sum, row_squares = lax.psum(
        (jnp.sum(hidden, axis=0), jnp.sum(hidden * hidden, axis=0)), "feat"
    )
    row_mean = row_sum / hid_total
    spread = row_squares / hid_total - row_mean * row_mean
    normed = (hidden - row_mean[None, :]) * lax.rsqrt(spread + 1e-05)[None, :] * norm_gain[:, None]
    return jax.nn.silu(normed).T.astype(jnp.bfloat16)


def solution(mesh):
    in_specs = (
        P("feat", "batch", None, None),
        P("feat", "batch", None, None),
        P("feat", "batch", None),
        P(),
        P("feat", None, None),
        P("feat", None, None, None),
        P(),
        P("feat"),
    )
    out_specs = P("batch", "feat")
    return jax.shard_map(body, mesh=mesh, in_specs=in_specs, out_specs=out_specs, check_vma=False)
```

profile of v0, /device:TPU:8, one launch (start us, length us, event | category | flops | bytes accessed | tf_op | source)
XLA Modules:
  0.0 1334.6 jit_solution(744671372483452733)
XLA Ops:
  6.5 1.8 fusion.15
  8.3 0.2 fusion.12
  8.7 0.2 fusion.10
  9.1 2.7 copy.38
  11.9 161.2 %gather_fusion.3 = bf16[16384,192]{1,0:T(8,128)(2,1)} fusion(bf16[2,2048,192]{2,1,0:T(8,128)(2,1)S(1)} %bitcast.104, s32[16384]{0:T(1024)S(1)} %bitcast.108), kind=kCustom, calls=%fused_computation.2.clone | custom fusion | bytes 12713984 | tf_op jit(solution)/shard_map/vmap(jit(_take))/gather | solution.py:8
  173.1 161.2 %gather_fusion.4 = bf16[16384,192]{1,0:T(8,128)(2,1)} fusion(bf16[2,2048,192]{2,1,0:T(8,128)(2,1)S(1)} %bitcast.105, s32[16384]{0:T(1024)S(1)} %bitcast.109), kind=kCustom, calls=%fused_computation.3.clone | custom fusion | bytes 12713984 | tf_op jit(solution)/shard_map/vmap(jit(_take))/gather | solution.py:8
  334.3 161.1 %gather_fusion.1 = bf16[16384,192]{1,0:T(8,128)(2,1)} fusion(bf16[2,2048,192]{2,1,0:T(8,128)(2,1)S(1)} %bitcast.106, s32[16384]{0:T(1024)S(1)} %bitcast.111), kind=kCustom, calls=%fused_computation.clone | custom fusion | bytes 12713984 | tf_op jit(solution)/shard_map/vmap(jit(_take))/gather | solution.py:8
  495.4 161.2 %gather_fusion.2 = bf16[16384,192]{1,0:T(8,128)(2,1)} fusion(bf16[2,2048,192]{2,1,0:T(8,128)(2,1)S(1)} %bitcast.107, s32[16384]{0:T(1024)S(1)} %bitcast.110), kind=kCustom, calls=%fused_computation.1.clone | custom fusion | bytes 12713984 | tf_op jit(solution)/shard_map/vmap(jit(_take))/gather | solution.py:8
  656.6 1.7 copy.37
  658.3 1.7 copy.41
  660.1 1.7 copy.44
  661.8 2.2 copy.47
  664.2 2.2 copy.36
  666.3 2.1 copy.40
  668.5 2.1 copy.43
  670.6 2.2 copy.46
  672.8 79.1 %add_convert_fusion = bf16[2,8192,192]{2,0,1:T(2,128)(2,1)S(1)} fusion(pred[2,8192]{0,1:T(8,128)(4,1)} %copy.46, pred[2,8192]{0,1:T(8,128)(4,1)} %copy.43, pred[2,8192]{0,1:T(8,128)(4,1)} %copy.40, pred[2,8192]{0,1:T(8,128)(4,1)} %copy.36, pred[2,8192]{0,1:T(8,128)(4,1)S(1)} %copy.37, pred[2,8192]{0,1:T(8,128)(4,1)S(1)} %copy.41, ...), kind=kLoop, calls=%fused_computation.5 | loop fusion | flops 50331648 | bytes 31588352 | tf_op jit(solution)/shard_map/convert_element_type | solution.py:42
  751.8 196.1 %all_to_all.18 = bf16[2,8192,192]{2,0,1:T(2,128)(2,1)} all-to-all(bf16[2,8192,192]{2,0,1:T(2,128)(2,1)S(1)} %add_convert_fusion), channel_id=1, replica_groups=mesh['batch'=64,'feat'=4] {'batch'}, dimensions={1} | all-to-all | bytes 12582912 | tf_op jit(solution)/shard_map/all_to_all | solution.py:43
  948.0 20.4 %copy.56 = bf16[2,64,128,192]{2,3,0,1:T(8,128)(2,1)} copy(bf16[2,64,128,192]{3,0,2,1:T(2,128)(2,1)} %bitcast.113) | data formatting | bytes 12582912 | tf_op jit(solution)/shard_map/all_to_all | solution.py:43
  968.4 0.2 reduce-scatter.2.cloned.1.call-start
  969.1 224.3 %all-gather.2.cloned.1.call-done = bf16[512,128,192]{1,2,0:T(8,128)(2,1)} async-done(((bf16[128,128,192]{1,2,0:T(8,128)(2,1)}), bf16[512,128,192]{1,2,0:T(8,128)(2,1)}) %all-gather.2.cloned.1.call-update) | async-done | bytes 25165840 | tf_op jit(solution)/shard_map/all_gather | solution.py:49
  1193.3 18.8 %gather_fusion = bf16[256,128,192]{1,2,0:T(8,128)(2,1)} fusion(bf16[512,128,192]{1,2,0:T(8,128)(2,1)} %all-gather.2.cloned.1.call-done, s32[1024]{0:T(1024)S(1)} %pad_clamp_fusion), kind=kCustom, calls=%fused_computation.4 | custom fusion | bytes 25166848 | tf_op jit(solution)/shard_map/jit(_take)/gather | solution.py:15
  1212.1 27.1 %copy.51 = bf16[4,2,32,128,192]{4,2,3,0,1:T(8,128)(2,1)} copy(bf16[4,2,32,128,192]{3,4,2,1,0:T(8,128)(2,1)} %bitcast.112) | data formatting | bytes 25165824 | tf_op jit(solution)/shard_map/jit(_take)/gather | solution.py:15
  1239.3 14.1 %broadcast_select_fusion.4 = bf16[4,2,32,128,192]{4,2,3,0,1:T(8,128)(2,1)} fusion(bf16[4,2,32,128,192]{4,2,3,0,1:T(8,128)(2,1)} %copy.51, pred[4,2,32]{2,0,1:T(4,128)(4,1)S(1)} %copy.35), kind=kLoop, calls=%fused_computation.10 | loop fusion | flops 6291456 | bytes 25166080 | tf_op jit(solution)/shard_map/jit(_take)/select_n | solution.py:15
  1253.4 11.3 broadcast_multiply_fusion
  1264.7 11.9 fusion.6
  1276.6 6.1 convolution_bitcast_fusion
  1282.7 0.7 dynamic_slice.7
  1283.4 32.5 %reduce-scatter.2.cloned.1.call-done = f32[1024,128]{0,1:T(8,128)} async-done(((f32[4096,128]{0,1:T(8,128)}), f32[1024,128]{0,1:T(8,128)}) %reduce-scatter.2.cloned.1.call-update) | async-done | bytes 524304 | tf_op jit(solution)/shard_map/reduce_scatter | solution.py:56
  1315.9 1.2 add_reduce_fusion
  1317.1 8.6 all-reduce
  1325.7 2.0 fusion.9
  (27 shorter events, 1.0 us)
Async XLA Ops:
  6.5 1258.2 %copy-start = (bf16[4,32,8]{1,2,0:T(8,128)(2,1)S(1)}, bf16[4,32,8]{1,2,0:T(8,128)(2,1)}, u32[]{:S(2)}) copy-start(bf16[4,32,8]{1,2,0:T(8,128)(2,1)} %param.14) | copy-start | bytes 6148
  6.5 1186.8 %all-gather.2.cloned.1.call-start = ((), (), s32[]{:S(2)}) async-start(), calls=%async_computation.2 | async-start | bytes 31457280 | tf_op jit(solution)/shard_map/all_gather | solution.py:49
  495.4 168.6 %copy-start.1 = (s32[1,2,8192]{2,1,0:T(2,128)S(1)}, s32[1,2,8192]{2,1,0:T(2,128)}, u32[]{:S(2)}) copy-start(s32[1,2,8192]{2,1,0:T(2,128)} %param.12) | copy-start | bytes 196612
  948.0 20.6 %copy-start.3 = (s32[16,2]{0,1:T(2,128)S(1)}, s32[16,2]{0,1:T(2,128)}, u32[]{:S(2)}) copy-start(s32[16,2]{0,1:T(2,128)} %param.13) | copy-start | bytes 388
  968.4 347.6 %reduce-scatter.2.cloned.1.call-start = ((), (), s32[]{:S(2)}) async-start(), calls=%async_computation.3 | async-start | bytes 2621440 | tf_op jit(solution)/shard_map/reduce_scatter | solution.py:56
  1276.6 49.1 %copy-start.2 = (f32[1024]{0:T(1024)S(1)}, f32[1024]{0:T(1024)}, u32[]{:S(2)}) copy-start(f32[1024]{0:T(1024)} %param.17) | copy-start | bytes 12292
Sparse Core Ops, SparseCore 0:
  968.5 224.7 all-gather.1
  1282.8 33.0 reduce-scatter.1
where the time goes:
time: 1340 us; the launch traced here: 1330 us
  local copies, waits for them, and re-layouts  732 us (55%)
  waiting for transfers between devices  257 us (19%)
  blocking collectives  205 us (15%)
  other arithmetic  97.5 us (7%)
  matrix products  29.3 us (2%)
  between operations  13.6 us (1%)
    gather x4, local copies, waits for them, and re-layouts, take_rows(): return jnp.take(table_one, ids_one, axis=0)  645 us
    all_gather x1, waiting for transfers between devices, body(): everything = lax.all_gather(feature_tile, 'feat', axis=0, tiled=True)  224 us
    all_to_all x1, blocking collectives, body(): lax.all_to_all(pooled, 'batch', split_axis=1, concat_axis=0, tiled=True)  196 us
    convert_element_type x1, other arithmetic, body(): pooled = pooled_sum.astype(jnp.bfloat16)  79.1 us
    gather x2, local copies, waits for them, and re-layouts, select_groups(): return jnp.take(source, wanted.reshape(-1), axis=0).reshape(shape_out)  45.9 us
    reduce_scatter x1, waiting for transfers between devices, body(): lax.psum_scatter(lax.dot_general(w_flat, squeezed, (((0,), (1,)), ((), ()...  32.5 us
  transfers between devices with their start and end apart: 2, of which 2 were waited for; matrix products, arithmetic and copies ran while one was open for 0% of the time, Pallas kernels for 0%

commit v1 on v0

--- a/solution.py
+++ b/solution.py
@@ -46,7 +46,9 @@
     group_size = compress.shape[1]
     first_pair = lax.axis_index("feat") * pair_count
     local_pairs = lax.dynamic_slice_in_dim(pair_groups, first_pair, pair_count, 0)
-    everything = lax.all_gather(feature_tile, "feat", axis=0, tiled=True)
+    everything = jnp.concatenate(
+        lax.all_to_all(jnp.stack([feature_tile] * lax.axis_size("feat")), "feat", 0, 0), axis=0
+    )
     squeezed = squeeze_pairs(select_groups(everything, local_pairs, group_size), compress)
     squeezed = squeezed.reshape(samples, -1)
     w_flat = w_hidden.reshape(-1, w_hidden.shape[3])

time: 1340 us -> 1410 us (1.052)
  waiting for transfers between devices: 257 us -> 302 us
  local copies, waits for them, and re-layouts: 732 us -> 748 us
    all_to_all x0 -> x1, waiting for transfers between devices: none -> 274 us  [body(): lax.all_to_all(jnp.stack([feature_tile] * lax.axis_size('feat')), 'feat',...]
    all_gather x1 -> x0, waiting for transfers between devices: 224 us -> none  [body(): everything = lax.all_gather(feature_tile, 'feat', axis=0, tiled=True)]
where the time goes in v1:
time: 1410 us; the launch traced here: 1400 us
  local copies, waits for them, and re-layouts  748 us (53%)
  waiting for transfers between devices  302 us (21%)
  blocking collectives  205 us (15%)
  other arithmetic  97.5 us (7%)
  matrix products  29.3 us (2%)
    gather x4, local copies, waits for them, and re-layouts, take_rows(): return jnp.take(table_one, ids_one, axis=0)  649 us
    all_to_all x1, waiting for transfers between devices, body(): lax.all_to_all(jnp.stack([feature_tile] * lax.axis_size('feat')), 'feat',...  274 us
    all_to_all x1, blocking collectives, body(): lax.all_to_all(pooled, 'batch', split_axis=1, concat_axis=0, tiled=True)  196 us
    convert_element_type x1, other arithmetic, body(): pooled = pooled_sum.astype(jnp.bfloat16)  79.1 us
    gather x2, local copies, waits for them, and re-layouts, select_groups(): return jnp.take(source, wanted.reshape(-1), axis=0).reshape(shape_out)  45.9 us
  transfers between devices with their start and end apart: 2, of which 2 were waited for; matrix products, arithmetic and copies ran while one was open for 0% of the time, Pallas kernels for 0%

profile of v1, /device:TPU:8, one launch (start us, length us, event | category | flops | bytes accessed | tf_op | source)
XLA Modules:
  0.0 1403.2 jit_solution(12250282406190803289)
XLA Ops:
  6.5 1.6 fusion.15
  8.1 0.2 fusion.12
  8.9 2.7 copy.51
  11.7 162.3 %gather_fusion.3 = bf16[16384,192]{1,0:T(8,128)(2,1)} fusion(bf16[2,2048,192]{2,1,0:T(8,128)(2,1)S(1)} %bitcast.105, s32[16384]{0:T(1024)S(1)} %bitcast.109), kind=kCustom, calls=%fused_computation.2.clone | custom fusion | bytes 12713984 | tf_op jit(solution)/shard_map/vmap(jit(_take))/gather | solution.py:8
  174.0 162.3 %gather_fusion.4 = bf16[16384,192]{1,0:T(8,128)(2,1)} fusion(bf16[2,2048,192]{2,1,0:T(8,128)(2,1)S(1)} %bitcast.106, s32[16384]{0:T(1024)S(1)} %bitcast.110), kind=kCustom, calls=%fused_computation.3.clone | custom fusion | bytes 12713984 | tf_op jit(solution)/shard_map/vmap(jit(_take))/gather | solution.py:8
  336.3 162.3 %gather_fusion.1 = bf16[16384,192]{1,0:T(8,128)(2,1)} fusion(bf16[2,2048,192]{2,1,0:T(8,128)(2,1)S(1)} %bitcast.107, s32[16384]{0:T(1024)S(1)} %bitcast.112), kind=kCustom, calls=%fused_computation.clone | custom fusion | bytes 12713984 | tf_op jit(solution)/shard_map/vmap(jit(_take))/gather | solution.py:8
  498.6 162.3 %gather_fusion.2 = bf16[16384,192]{1,0:T(8,128)(2,1)} fusion(bf16[2,2048,192]{2,1,0:T(8,128)(2,1)S(1)} %bitcast.108, s32[16384]{0:T(1024)S(1)} %bitcast.111), kind=kCustom, calls=%fused_computation.1.clone | custom fusion | bytes 12713984 | tf_op jit(solution)/shard_map/vmap(jit(_take))/gather | solution.py:8
  660.8 1.7 copy.50
  662.5 1.7 copy.54
  664.3 1.7 copy.57
  666.0 2.2 copy.60
  668.4 2.2 copy.49
  670.5 2.1 copy.53
  672.7 2.1 copy.56
  674.8 2.2 copy.59
  677.0 79.1 %add_convert_fusion = bf16[2,8192,192]{2,0,1:T(2,128)(2,1)S(1)} fusion(pred[2,8192]{0,1:T(8,128)(4,1)} %copy.59, pred[2,8192]{0,1:T(8,128)(4,1)} %copy.56, pred[2,8192]{0,1:T(8,128)(4,1)} %copy.53, pred[2,8192]{0,1:T(8,128)(4,1)} %copy.49, pred[2,8192]{0,1:T(8,128)(4,1)S(1)} %copy.50, pred[2,8192]{0,1:T(8,128)(4,1)S(1)} %copy.54, ...), kind=kLoop, calls=%fused_computation.5 | loop fusion | flops 50331648 | bytes 31588352 | tf_op jit(solution)/shard_map/convert_element_type | solution.py:42
  756.0 196.1 %all_to_all.20 = bf16[2,8192,192]{2,0,1:T(2,128)(2,1)} all-to-all(bf16[2,8192,192]{2,0,1:T(2,128)(2,1)S(1)} %add_convert_fusion), channel_id=1, replica_groups=mesh['batch'=64,'feat'=4] {'batch'}, dimensions={1} | all-to-all | bytes 12582912 | tf_op jit(solution)/shard_map/all_to_all | solution.py:43
  952.2 20.4 %copy.69 = bf16[2,64,128,192]{2,3,0,1:T(8,128)(2,1)} copy(bf16[2,64,128,192]{3,0,2,1:T(2,128)(2,1)} %bitcast.114) | data formatting | bytes 12582912 | tf_op jit(solution)/shard_map/all_to_all | solution.py:43
  972.6 11.1 stack.10
  983.7 8.7 all-to-all-start.1
  993.0 273.8 %all-to-all-done.1 = bf16[4,128,128,192]{2,3,1,0:T(8,128)(2,1)} async-done(((bf16[4,128,128,192]{2,3,1,0:T(8,128)(2,1)}), bf16[4,128,128,192]{2,3,1,0:T(8,128)(2,1)}, u32[]{:S(2)}, u32[]{:S(2)}) %all-to-all-start.1) | async-done | bytes 25165856 | tf_op jit(solution)/shard_map/all_to_all | solution.py:50
  1266.7 18.8 %gather_fusion = bf16[256,128,192]{1,2,0:T(8,128)(2,1)} fusion(bf16[512,128,192]{1,2,0:T(8,128)(2,1)} %bitcast.18, s32[1024]{0:T(1024)S(1)} %pad_clamp_fusion), kind=kCustom, calls=%fused_computation.4 | custom fusion | bytes 25166848 | tf_op jit(solution)/shard_map/jit(_take)/gather | solution.py:15
  1285.5 27.1 %copy.64 = bf16[4,2,32,128,192]{4,2,3,0,1:T(8,128)(2,1)} copy(bf16[4,2,32,128,192]{3,4,2,1,0:T(8,128)(2,1)} %bitcast.113) | data formatting | bytes 25165824 | tf_op jit(solution)/shard_map/jit(_take)/gather | solution.py:15
  1312.6 14.1 %broadcast_select_fusion.4 = bf16[4,2,32,128,192]{4,2,3,0,1:T(8,128)(2,1)} fusion(bf16[4,2,32,128,192]{4,2,3,0,1:T(8,128)(2,1)} %copy.64, pred[4,2,32]{2,0,1:T(4,128)(4,1)S(1)} %copy.48), kind=kLoop, calls=%fused_computation.10 | loop fusion | flops 6291456 | bytes 25166080 | tf_op jit(solution)/shard_map/jit(_take)/select_n | solution.py:15
  1326.8 11.4 broadcast_multiply_fusion
  1338.1 11.9 fusion.6
  1350.0 6.1 convolution_bitcast_fusion
  1356.1 0.7 dynamic_slice.7
  1356.8 27.7 %reduce-scatter.2.cloned.1.call-done = f32[1024,128]{0,1:T(8,128)} async-done(((f32[4096,128]{0,1:T(8,128)}), f32[1024,128]{0,1:T(8,128)}) %reduce-scatter.2.cloned.1.call-update) | async-done | bytes 524304 | tf_op jit(solution)/shard_map/reduce_scatter | solution.py:58
  1384.5 1.2 add_reduce_fusion
  1385.7 8.6 all-reduce
  1394.3 2.0 fusion.9
  (27 shorter events, 1.2 us)
Async XLA Ops:
  6.5 1331.6 %copy-start = (bf16[4,32,8]{1,2,0:T(8,128)(2,1)S(1)}, bf16[4,32,8]{1,2,0:T(8,128)(2,1)}, u32[]{:S(2)}) copy-start(bf16[4,32,8]{1,2,0:T(8,128)(2,1)} %param.14) | copy-start | bytes 6148
  498.6 169.7 %copy-start.1 = (s32[1,2,8192]{2,1,0:T(2,128)S(1)}, s32[1,2,8192]{2,1,0:T(2,128)}, u32[]{:S(2)}) copy-start(s32[1,2,8192]{2,1,0:T(2,128)} %param.12) | copy-start | bytes 196612
  983.7 8.8 copy-start.3
  983.7 283.0 %all-to-all-start.1 = ((bf16[4,128,128,192]{2,3,1,0:T(8,128)(2,1)}), bf16[4,128,128,192]{2,3,1,0:T(8,128)(2,1)}, u32[]{:S(2)}, u32[]{:S(2)}) async-start(bf16[4,128,128,192]{2,3,1,0:T(8,128)(2,1)} %stack.10), calls=%async_computation.1 | async-start | bytes 50331648 | tf_op jit(solution)/shard_map/all_to_all | solution.py:50
  992.5 392.1 %reduce-scatter.2.cloned.1.call-start = ((), (), s32[]{:S(2)}) async-start(), calls=%async_computation.3 | async-start | bytes 2621440 | tf_op jit(solution)/shard_map/reduce_scatter | solution.py:58
  1350.0 44.3 %copy-start.2 = (f32[1024]{0:T(1024)S(1)}, f32[1024]{0:T(1024)}, u32[]{:S(2)}) copy-start(f32[1024]{0:T(1024)} %param.17) | copy-start | bytes 12292
Sparse Core Ops, SparseCore 0:
  1356.2 28.2 reduce-scatter.1
